TPU v7x, 32 devices: a whole 2x2x4 slice. The times are simulated.
32 devices in a mesh: tile: 8 (over z, y), ka: 4 (over x, core).
Axes of the slice: x: 2, y: 2, z: 4, core: 2. Of those that a mesh axis runs over, the one named last changes fastest.
Arguments:
- integrals: bfloat16 [640, 48, 640], P('tile', 'ka'), may hold values from -0.03125 to 0.03125
- amplitudes: bfloat16 [48, 640, 8, 640], P('ka', 'tile'), may hold values from -24 to 24
- virt_energy: float32 [640], replicated, may hold values from 0.5 to 3
- pair_energy: float32 [8], replicated, may hold values from -6 to -1
Outputs:
- update: bfloat16 [8, 640, 640], P('ka', 'tile')
All inputs are finite; a program needn't handle non-finite values.
Results may differ from a plain program's by a relative error of at most 0.001.
Values may be sent and summed in bfloat16 or wider, within the bound.
No kernel may reach another device: no remote copies, remote signals or barrier semaphores. Data moves between devices by JAX's collectives and lax.ppermute only.
A program may use at most 128 MiB of HBM per device.

v0:
```python
import jax
import jax.numpy as jnp
from jax import lax
from jax.sharding import PartitionSpec as P


def per_device(integrals, amplitudes, virt_energy, pair_energy):
    particle_hole = lax.all_to_all(amplitudes, "tile", split_axis=3, concat_axis=1, tiled=True)
    pair_count = particle_hole.shape[2]
    col_count = particle_hole.shape[3]
    summed = jnp.einsum(
        "cka,kcjb->jab",
        lax.all_gather(integrals, "tile", axis=0, tiled=True),
        particle_hole,
        preferred_element_type=jnp.float32,
    )
    tile_pos = lax.axis_index("tile")
    ka_pos = lax.axis_index("ka")
    local_pairs = pair_count // lax.axis_size("ka")
    own_virt = lax.dynamic_slice_in_dim(virt_energy, tile_pos * col_count, col_count, 0)
    own_pairs = lax.dynamic_slice_in_dim(pair_energy, ka_pos * local_pairs, local_pairs, 0)
    regrouped = lax.all_to_all(summed, "tile", split_axis=1, concat_axis=2, tiled=True)
    reduced = lax.psum_scatter(regrouped, "ka", scatter_dimension=0, tiled=True)
    denominator = own_virt[None, :, None] + virt_energy[None, None, :] - own_pairs[:, None, None]
    return (reduced / denominator).astype(jnp.bfloat16)


def solution(mesh):
    in_specs = (P("tile", "ka", None), P("ka", "tile", None, None), P(), P())
    out_specs = P("ka", "tile", None)
    return jax.shard_map(
        per_device, mesh=mesh, in_specs=in_specs, out_specs=out_specs, check_vma=False
    )
```

profile of v0, /device:TPU:0, one launch (start us, length us, event | category | flops | bytes accessed | tf_op | source)
XLA Modules:
  0.0 652.1 jit_solution(2694304044166551413)
XLA Ops:
  6.5 20.2 %copy.11 = bf16[12,80,8,640]{1,2,0,3:T(8,128)(2,1)} copy(bf16[12,80,8,640]{3,2,1,0:T(8,128)(2,1)} %param.5) | data formatting | bytes 19660800 | tf_op args[1]
  26.7 7.3 %all-to-all-start = ((bf16[12,80,8,640]{1,2,0,3:T(8,128)(2,1)}), bf16[12,80,8,640]{1,2,0,3:T(8,128)(2,1)}, u32[]{:S(2)}, u32[]{:S(2)}) async-start(bf16[12,80,8,640]{1,2,0,3:T(8,128)(2,1)} %copy.11), calls=%async_computation | async-start | bytes 31457280 | tf_op jit(solution)/shard_map/all_to_all | solution.py:8
  34.0 0.0 all-gather.2.cloned.1.call-start
  34.1 0.7 all-gather.2.cloned.1.call-update
  34.8 0.0 reduce-scatter.2.cloned.1.call-start
  34.8 458.2 %all-to-all-done = bf16[12,80,8,640]{1,2,0,3:T(8,128)(2,1)} async-done(((bf16[12,80,8,640]{1,2,0,3:T(8,128)(2,1)}), bf16[12,80,8,640]{1,2,0,3:T(8,128)(2,1)}, u32[]{:S(2)}, u32[]{:S(2)}) %all-to-all-start) | async-done | bytes 9830432 | tf_op jit(solution)/shard_map/all_to_all | solution.py:8
  493.0 17.9 %copy.17 = bf16[12,80,8,8,80]{1,3,4,0,2:T(8,128)(2,1)} copy(bf16[12,80,8,8,80]{1,2,0,4,3:T(8,128)(2,1)} %bitcast) | data formatting | bytes 19660800 | tf_op jit(solution)/shard_map/all_to_all | solution.py:8
  510.8 23.0 %all_to_all.29 = bf16[12,640,8,80]{1,3,0,2:T(8,128)(2,1)} reshape(bf16[12,8,80,8,80]{2,1,4,0,3:T(8,128)(2,1)} %bitcast.24) | data formatting | bytes 19660800 | tf_op jit(solution)/shard_map/all_to_all | solution.py:8
  533.9 0.0 all-gather.2.cloned.1.call-done
  533.9 13.0 %fusion.2 = f32[8,640,80]{1,2,0:T(8,128)} fusion(bf16[12,640,8,80]{1,3,0,2:T(8,128)(2,1)} %all_to_all.29, bf16[640,12,640]{2,0,1:T(8,128)(2,1)} %all-gather.2.cloned.1.call-done), kind=kOutput, calls=%fused_computation.3 | convolution fusion | flops 6291456000 | bytes 21299200 | tf_op jit(solution)/shard_map/cka,kcjb->jab/dot_general | solution.py:11
  546.9 0.0 copy-start.1
  546.9 0.0 copy-start
  546.9 2.4 copy.13
  549.3 63.0 %all_to_all.36 = f32[8,640,80]{2,0,1:T(8,128)S(1)} all-to-all(f32[8,640,80]{2,0,1:T(8,128)S(1)} %copy.13), channel_id=1, replica_groups=mesh['tile'=8,'ka'=4] {'tile'}, dimensions={1} | all-to-all | bytes 3276800 | tf_op jit(solution)/shard_map/all_to_all | solution.py:22
  612.4 1.5 copy.14
  613.9 1.7 all_to_all.33
  615.6 0.0 reduce-scatter.2.cloned.1.call-update
  615.7 0.0 copy-done.1
  615.7 0.1 dynamic_slice.7
  615.8 0.0 copy-done
  615.8 0.1 dynamic_slice.6
  615.8 0.1 broadcast_add_fusion
  615.9 27.5 %reduce-scatter.2.cloned.1.call-done = f32[2,80,640]{2,1,0:T(8,128)} async-done(((f32[8,80,640]{2,1,0:T(8,128)}), f32[2,80,640]{2,1,0:T(8,128)}) %reduce-scatter.2.cloned.1.call-update) | async-done | bytes 409616 | tf_op jit(solution)/shard_map/reduce_scatter | solution.py:23
  643.5 1.8 divide_convert_fusion
Async XLA Ops:
  26.7 466.2 %all-to-all-start = ((bf16[12,80,8,640]{1,2,0,3:T(8,128)(2,1)}), bf16[12,80,8,640]{1,2,0,3:T(8,128)(2,1)}, u32[]{:S(2)}, u32[]{:S(2)}) async-start(bf16[12,80,8,640]{1,2,0,3:T(8,128)(2,1)} %copy.11), calls=%async_computation | async-start | bytes 31457280 | tf_op jit(solution)/shard_map/all_to_all | solution.py:8
  34.0 499.9 %all-gather.2.cloned.1.call-start = ((), (), s32[]{:S(2)}) async-start(), calls=%async_computation.3 | async-start | bytes 11059200 | tf_op jit(solution)/shard_map/all_gather | solution.py:13
  34.8 608.7 %reduce-scatter.2.cloned.1.call-start = ((), (), s32[]{:S(2)}) async-start(), calls=%async_computation.4 | async-start | bytes 2048000 | tf_op jit(solution)/shard_map/reduce_scatter | solution.py:23
  546.9 68.8 %copy-start.1 = (f32[8]{0:T(128)S(1)}, f32[8]{0:T(128)}, u32[]{:S(2)}) copy-start(f32[8]{0:T(128)} %param.7) | copy-start | bytes 100
  546.9 68.9 %copy-start = (f32[640]{0:T(1024)S(1)}, f32[640]{0:T(1024)}, u32[]{:S(2)}) copy-start(f32[640]{0:T(1024)} %param.6) | copy-start | bytes 7684
Sparse Core Ops, SparseCore 0:
  37.1 412.8 all-gather.1
  615.8 27.6 reduce-scatter.1
where the time goes:
time: 654 us; the launch traced here: 652 us
  waiting for transfers between devices  486 us (74%)
  local copies, waits for them, and re-layouts  67 us (10%)
  blocking collectives  63 us (10%)
  between operations  13.4 us (2%)
  matrix products  13 us (2%)
  starting transfers between devices  7.36 us (1%)
    all_to_all x1, waiting for transfers between devices, per_device(): lax.all_to_all(amplitudes, 'tile', split_axis=3, concat_axis=1, tiled=True)  458 us
    all_to_all x1, blocking collectives, per_device(): lax.all_to_all(summed, 'tile', split_axis=1, concat_axis=2, tiled=True)  63 us
    all_to_all x2, local copies, waits for them, and re-layouts, per_device(): lax.all_to_all(amplitudes, 'tile', split_axis=3, concat_axis=1, tiled=True)  40.9 us
    reduce_scatter x1, waiting for transfers between devices, per_device(): reduced = lax.psum_scatter(regrouped, 'ka', scatter_dimension=0, tiled=True)  27.5 us
    unnamed x5, local copies, waits for them, and re-layouts  20.2 us
  transfers between devices with their start and end apart: 3, of which 2 were waited for; matrix products, arithmetic and copies ran while one was open for 3% of the time, Pallas kernels for 0%

commit v1 on v0

--- a/solution.py
+++ b/solution.py
@@ -2,6 +2,18 @@
 import jax.numpy as jnp
 from jax import lax
 from jax.sharding import PartitionSpec as P
+
+
+def in_blocks(x, dim, size):
+    shape = x.shape
+    tiles = x.reshape(*shape[:dim], size, shape[dim] // size, *shape[dim + 1 :])
+    return jnp.moveaxis(tiles, dim, 0)
+
+
+def in_order(parts, dim):
+    parts = jnp.moveaxis(parts, 0, dim)
+    dims = parts.shape
+    return parts.reshape(*dims[:dim], dims[dim] * dims[dim + 1], *dims[dim + 2 :])
 
 
 def per_device(integrals, amplitudes, virt_energy, pair_energy):
@@ -19,7 +31,14 @@
     local_pairs = pair_count // lax.axis_size("ka")
     own_virt = lax.dynamic_slice_in_dim(virt_energy, tile_pos * col_count, col_count, 0)
     own_pairs = lax.dynamic_slice_in_dim(pair_energy, ka_pos * local_pairs, local_pairs, 0)
-    regrouped = lax.all_to_all(summed, "tile", split_axis=1, concat_axis=2, tiled=True)
+    size, position = (lax.axis_size("tile"), lax.axis_index("tile"))
+    blocks = in_blocks(summed, 1, size)
+    outs = [blocks[position]]
+    for step in range(1, size):
+        sent = blocks[position ^ step]
+        outs.append(lax.ppermute(sent, "tile", [(i, i ^ step) for i in range(size)]))
+    blocks = jnp.stack(outs)[position ^ jnp.arange(size)]
+    regrouped = in_order(blocks, 2)
     reduced = lax.psum_scatter(regrouped, "ka", scatter_dimension=0, tiled=True)
     denominator = own_virt[None, :, None] + virt_energy[None, None, :] - own_pairs[:, None, None]
     return (reduced / denominator).astype(jnp.bfloat16)

time: 654 us -> 668 us (1.021)
  blocking collectives: 63 us -> 0 us
  waiting for transfers between devices: 486 us -> 530 us
  local copies, waits for them, and re-layouts: 67 us -> 90.7 us
  starting transfers between devices: 7.36 us -> 16.3 us
    all_to_all x1 -> x0, blocking collectives: 63 us -> none  [per_device(): lax.all_to_all(summed, 'tile', split_axis=1, concat_axis=2, tiled=True)]
    ppermute x0 -> x7, waiting for transfers between devices: none -> 35.1 us  [per_device(): lax.ppermute(sent, 'tile', [(i, i ^ step) for i in range(size)])]
    another operation x0 -> x10, local copies, waits for them, and re-layouts: none -> 10.5 us
    reduce_scatter x1, waiting for transfers between devices: 27.5 us -> 36.5 us  [per_device(): reduced = lax.psum_scatter(regrouped, 'ka', scatter_dimension=0, tiled=True)]
    ppermute x0 -> x7, starting transfers between devices: none -> 8.97 us  [per_device(): lax.ppermute(sent, 'tile', [(i, i ^ step) for i in range(size)])]
    unnamed x5 -> x16, local copies, waits for them, and re-layouts: 20.2 us -> 28.3 us
  transfers between devices with their start and end apart: 3 -> 10, of which waited for: 2 -> 5; matrix products, arithmetic and copies ran while one was open for 3% -> 4% of each run, Pallas kernels for 0% -> 0%
where the time goes in v1:
time: 668 us; the launch traced here: 666 us
  waiting for transfers between devices  530 us (79%)
  local copies, waits for them, and re-layouts  90.7 us (14%)
  starting transfers between devices  16.3 us (2%)
  between operations  13.6 us (2%)
  matrix products  13 us (2%)
    all_to_all x1, waiting for transfers between devices, per_device(): lax.all_to_all(amplitudes, 'tile', split_axis=3, concat_axis=1, tiled=True)  458 us
    all_to_all x2, local copies, waits for them, and re-layouts, per_device(): lax.all_to_all(amplitudes, 'tile', split_axis=3, concat_axis=1, tiled=True)  40.9 us
    reduce_scatter x1, waiting for transfers between devices, per_device(): reduced = lax.psum_scatter(regrouped, 'ka', scatter_dimension=0, tiled=True)  36.5 us
    ppermute x7, waiting for transfers between devices, per_device(): lax.ppermute(sent, 'tile', [(i, i ^ step) for i in range(size)])  35.1 us
    unnamed x16, local copies, waits for them, and re-layouts  28.3 us
  transfers between devices with their start and end apart: 10, of which 5 were waited for; matrix products, arithmetic and copies ran while one was open for 4% of the time, Pallas kernels for 0%

profile of v1, /device:TPU:0, one launch (start us, length us, event | category | flops | bytes accessed | tf_op | source)
XLA Modules:
  0.0 665.9 jit_solution(3112469908212230939)
XLA Ops:
  6.5 20.2 %copy.36 = bf16[12,80,8,640]{1,2,0,3:T(8,128)(2,1)} copy(bf16[12,80,8,640]{3,2,1,0:T(8,128)(2,1)} %param.5) | data formatting | bytes 19660800 | tf_op args[1]
  26.7 7.3 %all-to-all-start = ((bf16[12,80,8,640]{1,2,0,3:T(8,128)(2,1)}), bf16[12,80,8,640]{1,2,0,3:T(8,128)(2,1)}, u32[]{:S(2)}, u32[]{:S(2)}) async-start(bf16[12,80,8,640]{1,2,0,3:T(8,128)(2,1)} %copy.36), calls=%async_computation | async-start | bytes 31457280 | tf_op jit(solution)/shard_map/all_to_all | solution.py:20
  34.8 458.1 %all-to-all-done = bf16[12,80,8,640]{1,2,0,3:T(8,128)(2,1)} async-done(((bf16[12,80,8,640]{1,2,0,3:T(8,128)(2,1)}), bf16[12,80,8,640]{1,2,0,3:T(8,128)(2,1)}, u32[]{:S(2)}, u32[]{:S(2)}) %all-to-all-start) | async-done | bytes 9830432 | tf_op jit(solution)/shard_map/all_to_all | solution.py:20
  492.9 17.9 %copy.49 = bf16[12,80,8,8,80]{1,3,4,0,2:T(8,128)(2,1)} copy(bf16[12,80,8,8,80]{1,2,0,4,3:T(8,128)(2,1)} %bitcast) | data formatting | bytes 19660800 | tf_op jit(solution)/shard_map/all_to_all | solution.py:20
  510.8 23.1 %all_to_all.16 = bf16[12,640,8,80]{1,3,0,2:T(8,128)(2,1)} reshape(bf16[12,8,80,8,80]{2,1,4,0,3:T(8,128)(2,1)} %bitcast.49) | data formatting | bytes 19660800 | tf_op jit(solution)/shard_map/all_to_all | solution.py:20
  533.9 13.0 %fusion.2 = f32[8,640,80]{1,2,0:T(8,128)} fusion(bf16[12,640,8,80]{1,3,0,2:T(8,128)(2,1)} %all_to_all.16, bf16[640,12,640]{2,0,1:T(8,128)(2,1)} %all-gather.2.cloned.1.call-done), kind=kOutput, calls=%fused_computation.4 | convolution fusion | flops 6291456000 | bytes 21299200 | tf_op jit(solution)/shard_map/cka,kcjb->jab/dot_general | solution.py:23
  546.9 2.4 reshape.70
  549.2 3.2 constant_dynamic-slice_fusion
  553.6 1.9 copy.39
  556.9 1.8 copy.40
  559.9 2.1 collective-permute-start.2
  562.4 3.8 collective-permute-start.4
  567.3 1.5 collective-permute-start.5
  568.7 1.7 bitcast_dynamic-update-slice_fusion.6
  570.5 10.5 %collective-permute-done.1 = f32[8,80,80]{2,1,0:T(8,128)} collective-permute-done((f32[8,80,80]{2,1,0:T(8,128)}, f32[8,80,80]{2,1,0:T(8,128)}, u32[]{:S(2)}, u32[]{:S(2)}) %collective-permute-start.1) | collective-permute-done | bytes 204832 | tf_op jit(solution)/shard_map/ppermute | solution.py:39
  581.0 1.7 bitcast_dynamic-update-slice_fusion.5
  582.7 1.6 collective-permute-done.2
  584.3 1.7 bitcast_dynamic-update-slice_fusion.4
  586.7 23.0 %collective-permute-done.4 = f32[8,80,80]{2,1,0:T(8,128)S(1)} collective-permute-done((f32[8,80,80]{2,1,0:T(8,128)S(1)}, f32[8,80,80]{2,1,0:T(8,128)S(1)}, u32[]{:S(2)}, u32[]{:S(2)}) %collective-permute-start.4) | collective-permute-done | bytes 204832 | tf_op jit(solution)/shard_map/ppermute | solution.py:39
  612.0 2.5 gather_fusion
  614.4 3.0 copy.46
  617.5 3.0 reshape.71
  620.8 36.5 %reduce-scatter.2.cloned.1.call-done = f32[2,80,640]{2,1,0:T(8,128)} async-done(((f32[8,80,640]{2,1,0:T(8,128)}), f32[2,80,640]{2,1,0:T(8,128)}) %reduce-scatter.2.cloned.1.call-update) | async-done | bytes 409616 | tf_op jit(solution)/shard_map/reduce_scatter | solution.py:42
  657.3 1.8 divide_convert_fusion
  (37 shorter events, 9.1 us)
Async XLA Ops:
  26.7 466.2 %all-to-all-start = ((bf16[12,80,8,640]{1,2,0,3:T(8,128)(2,1)}), bf16[12,80,8,640]{1,2,0,3:T(8,128)(2,1)}, u32[]{:S(2)}, u32[]{:S(2)}) async-start(bf16[12,80,8,640]{1,2,0,3:T(8,128)(2,1)} %copy.36), calls=%async_computation | async-start | bytes 31457280 | tf_op jit(solution)/shard_map/all_to_all | solution.py:20
  34.0 499.9 %all-gather.2.cloned.1.call-start = ((), (), s32[]{:S(2)}) async-start(), calls=%async_computation.2 | async-start | bytes 11059200 | tf_op jit(solution)/shard_map/all_gather | solution.py:25
  34.7 622.6 %reduce-scatter.2.cloned.1.call-start = ((), (), s32[]{:S(2)}) async-start(), calls=%async_computation.3 | async-start | bytes 2048000 | tf_op jit(solution)/shard_map/reduce_scatter | solution.py:42
  552.4 9.6 %copy-start.1 = (f32[8,1,80,80]{2,1,3,0:T(1,128)S(1)}, f32[8,1,80,80]{2,1,3,0:T(1,128)}, u32[]{:S(2)}) copy-start(f32[8,1,80,80]{2,1,3,0:T(1,128)} %get-tuple-element.8) | copy-start | bytes 614404
  552.4 9.8 %copy-start = (f32[8,1,80,80]{2,1,3,0:T(1,128)S(1)}, f32[8,1,80,80]{2,1,3,0:T(1,128)}, u32[]{:S(2)}) copy-start(f32[8,1,80,80]{2,1,3,0:T(1,128)} %get-tuple-element.7) | copy-start | bytes 614404
  555.5 11.8 %collective-permute-start = (f32[8,80,80]{2,1,0:T(8,128)}, f32[8,80,80]{2,1,0:T(8,128)}, u32[]{:S(2)}, u32[]{:S(2)}) collective-permute-start(f32[8,80,80]{2,1,0:T(8,128)} %bitcast.7), channel_id=1, source_target_pairs={{0,4},{4,0},{8,12},{12,8},{16,20},{20,16},{24,28},{28,24},{1,5},{5... | collective-permute-start | bytes 614408 | tf_op jit(solution)/shard_map/ppermute | solution.py:39
  558.7 22.2 %collective-permute-start.1 = (f32[8,80,80]{2,1,0:T(8,128)}, f32[8,80,80]{2,1,0:T(8,128)}, u32[]{:S(2)}, u32[]{:S(2)}) collective-permute-start(f32[8,80,80]{2,1,0:T(8,128)} %bitcast.9), channel_id=1, source_target_pairs={{0,8},{4,12},{8,0},{12,4},{16,24},{20,28},{24,16},{28,20},{1,9},{5... | collective-permute-start | bytes 614408 | tf_op jit(solution)/shard_map/ppermute | solution.py:39
  559.9 24.4 %collective-permute-start.2 = (f32[8,80,80]{2,1,0:T(8,128)S(1)}, f32[8,80,80]{2,1,0:T(8,128)}, u32[]{:S(2)}, u32[]{:S(2)}) collective-permute-start(f32[8,80,80]{2,1,0:T(8,128)S(1)} %bitcast.55), channel_id=1, source_target_pairs={{0,12},{4,8},{8,4},{12,0},{16,28},{20,24},{24,20},{28,16},{1,13},{... | collective-permute-start | bytes 614408 | tf_op jit(solution)/shard_map/ppermute | solution.py:39
  562.1 23.9 %collective-permute-start.3 = (f32[8,80,80]{2,1,0:T(8,128)S(1)}, f32[8,80,80]{2,1,0:T(8,128)S(1)}, u32[]{:S(2)}, u32[]{:S(2)}) collective-permute-start(f32[8,80,80]{2,1,0:T(8,128)S(1)} %bitcast.54), channel_id=1, source_target_pairs={{0,16},{4,20},{8,24},{12,28},{16,0},{20,4},{24,8},{28,12},{1,17},{... | collective-permute-start | bytes 614408 | tf_op jit(solution)/shard_map/ppermute | solution.py:39
  562.4 47.4 %collective-permute-start.4 = (f32[8,80,80]{2,1,0:T(8,128)S(1)}, f32[8,80,80]{2,1,0:T(8,128)S(1)}, u32[]{:S(2)}, u32[]{:S(2)}) collective-permute-start(f32[8,80,80]{2,1,0:T(8,128)S(1)} %bitcast.53), channel_id=1, source_target_pairs={{0,20},{4,16},{8,28},{12,24},{16,4},{20,0},{24,12},{28,8},{1,21},{... | collective-permute-start | bytes 614408 | tf_op jit(solution)/shard_map/ppermute | solution.py:39
  567.3 43.2 %collective-permute-start.5 = (f32[8,80,80]{2,1,0:T(8,128)S(1)}, f32[8,80,80]{2,1,0:T(8,128)S(1)}, u32[]{:S(2)}, u32[]{:S(2)}) collective-permute-start(f32[8,80,80]{2,1,0:T(8,128)S(1)} %bitcast.52), channel_id=1, source_target_pairs={{0,24},{4,28},{8,16},{12,20},{16,8},{20,12},{24,0},{28,4},{1,25},{... | collective-permute-start | bytes 614408 | tf_op jit(solution)/shard_map/ppermute | solution.py:39
  581.0 30.3 %collective-permute-start.6 = (f32[8,80,80]{2,1,0:T(8,128)S(1)}, f32[8,80,80]{2,1,0:T(8,128)S(1)}, u32[]{:S(2)}, u32[]{:S(2)}) collective-permute-start(f32[8,80,80]{2,1,0:T(8,128)S(1)} %bitcast.51), channel_id=1, source_target_pairs={{0,28},{4,24},{8,20},{12,16},{16,12},{20,8},{24,4},{28,0},{1,29},{... | collective-permute-start | bytes 614408 | tf_op jit(solution)/shard_map/ppermute | solution.py:39
  617.5 3.1 copy-start.3
  617.5 3.2 copy-start.2
Sparse Core Ops, SparseCore 0:
  37.1 412.8 all-gather.1
  620.6 36.5 reduce-scatter.1
